TPU v7x, 32 devices: a whole 2x2x4 slice. The times are simulated.
32 devices in a mesh: dp: 8 (over z, core), clus: 4 (over y, x).
Axes of the slice: x: 2, y: 2, z: 4, core: 2. Of those that a mesh axis runs over, the one named last changes fastest.
Arguments:
- rows: bfloat16 [8192, 1024], P(('dp', 'clus')), may hold values from -8 to 8
- fine_assign: int32 [8192], P(('dp', 'clus')), may hold values from 0 to 8191, as said below
- parent1: int32 [8192], P(('dp', 'clus')), may hold values from 0 to 2047, as said below
- parent2: int32 [2048], P('dp'), may hold values from 0 to 511
- parent3: int32 [512], replicated, may hold values from 0 to 63
- shrink: float32 [4], replicated, may hold values from 0.5 to 2
Outputs:
- fine_centroids: bfloat16 [8192, 1024], P(('dp', 'clus'))
- mid_centroids: bfloat16 [2048, 1024], P(('dp', 'clus'))
- coarse_centroids: bfloat16 [512, 1024], P(('dp', 'clus'))
- spread: float32 [8192], P(('dp', 'clus'))
Inputs may be any that keep to these rules, and one draw needn't show every extreme that they name: `fine_assign`: devices are numbered d = dp index * 4 + clus index, and fine centroid k is owned by device k // 256. Every row of device d names a fine centroid owned by a device of the same dp index. At most 128 rows of one device name centroids of one owner, and in every dp group some owner is named by exactly 128 rows of each device of the group. parent1[k] is one of the 256 second-level centroids g * 256 to g * 256 + 255, with g = k // 1024.
All inputs are finite; a program needn't handle non-finite values.
Results may differ from a plain program's by a relative error of at most 0.0035.
Values may be sent and summed in bfloat16 or wider, within the bound.
A program may use at most 64 MiB of HBM per device.

v0:
```python
import jax
import jax.numpy as jnp
from jax import lax
from jax.sharding import PartitionSpec as P

K4 = 64
HIGH = lax.Precision.HIGHEST


def shrunk(sums, counts, prior, weight):
    return (sums + weight * prior) / (counts + weight)[:, None]


def local(rows, fine_assign, parent1, parent2, parent3, shrink):
    groups = lax.axis_size("clus")
    dp_count = lax.axis_size("dp")
    devices = groups * dp_count
    clus_index = lax.axis_index("clus")
    dp_index = lax.axis_index("dp")
    count = rows.shape[0]
    width = rows.shape[1]
    fine_dev = parent1.shape[0]
    middle_dp = parent2.shape[0]
    third = parent3.shape[0]
    slots = 2 * count // groups
    total = count * devices
    weight_top = shrink[0] * (total / K4)
    weight_third = shrink[1] * (total / third)
    weight_middle = shrink[2] * (total / (middle_dp * dp_count))
    weight_fine = shrink[3] * (total / (fine_dev * devices))
    local_ids = fine_assign - dp_index * groups * fine_dev
    target = local_ids // fine_dev
    within = local_ids - target * fine_dev
    target_hot = (target[:, None] == jnp.arange(groups)[None, :]).astype(jnp.bfloat16)
    earlier = (jnp.arange(count)[:, None] > jnp.arange(count)[None, :]).astype(jnp.bfloat16)
    before = jnp.dot(earlier, target_hot, preferred_element_type=jnp.float32)
    rank = jnp.sum(before * target_hot.astype(jnp.float32), axis=1).astype(jnp.int32)
    slot_of = target * slots + rank
    source = (
        jnp.full((groups * slots,), count, jnp.int32)
        .at[slot_of]
        .set(jnp.arange(count, dtype=jnp.int32))
    )
    padded = jnp.concatenate([rows, jnp.zeros((1, width), jnp.bfloat16)], axis=0)
    send_rows = padded[source].reshape(groups, slots, width)
    send_ids = jnp.concatenate([within, jnp.full((1,), -1, jnp.int32)])[source].reshape(
        groups, slots
    )
    got_rows, got_ids = (
        lax.all_to_all(send_rows, "clus", split_axis=0, concat_axis=0, tiled=True),
        lax.all_to_all(send_ids, "clus", split_axis=0, concat_axis=0, tiled=True),
    )
    got_rows = got_rows.reshape(groups * slots, width)
    got_ids = got_ids.reshape(groups * slots)
    member = (got_ids[:, None] == jnp.arange(fine_dev)[None, :]).astype(jnp.bfloat16)
    contract = (((0,), (0,)), ((), ()))
    fine_sums = lax.dot_general(member, got_rows, contract, preferred_element_type=jnp.float32)
    fine_counts = jnp.sum(member.astype(jnp.float32), axis=0)
    middle_local = parent1 - dp_index * middle_dp
    child_hot = (jnp.arange(middle_dp)[:, None] == middle_local[None, :]).astype(jnp.float32)
    middle_part = jnp.dot(child_hot, fine_sums, precision=HIGH)
    middle_tally = jnp.dot(child_hot, fine_counts, precision=HIGH)
    share = middle_dp // groups
    offset = clus_index * share
    middle_sums, middle_counts = (
        lax.psum_scatter(middle_part, "clus", scatter_dimension=0, tiled=True),
        lax.psum_scatter(middle_tally, "clus", scatter_dimension=0, tiled=True),
    )
    own_parent2 = lax.dynamic_slice_in_dim(parent2, offset, share, 0)
    third_share = third // devices
    third_start = (dp_index * groups + clus_index) * third_share
    third_hot = (jnp.arange(third)[:, None] == own_parent2[None, :]).astype(jnp.float32)
    third_part = jnp.dot(third_hot, middle_sums, precision=HIGH)
    third_tally = jnp.dot(third_hot, middle_counts, precision=HIGH)
    third_sums, third_counts = lax.psum((third_part, third_tally), ("dp", "clus"))
    top_hot = (jnp.arange(K4)[:, None] == parent3[None, :]).astype(jnp.float32)
    top_sums = jnp.dot(top_hot, third_sums, precision=HIGH)
    top_counts = jnp.dot(top_hot, third_counts, precision=HIGH)
    center = jnp.sum(top_sums, axis=0) / total
    top_means = shrunk(top_sums, top_counts, center[None, :], weight_top)
    third_means = shrunk(
        third_sums, third_counts, jnp.dot(top_hot.T, top_means, precision=HIGH), weight_third
    )
    third_out = lax.dynamic_slice_in_dim(third_means, third_start, third_share, 0)
    parent_hot = (own_parent2[:, None] == jnp.arange(third)[None, :]).astype(jnp.float32)
    middle_out = shrunk(
        middle_sums, middle_counts, jnp.dot(parent_hot, third_means, precision=HIGH), weight_middle
    )
    middle_means = lax.all_gather(middle_out, "clus", axis=0, tiled=True)
    fine_means = shrunk(
        fine_sums, fine_counts, jnp.dot(child_hot.T, middle_means, precision=HIGH), weight_fine
    )
    fine_out = fine_means.astype(jnp.bfloat16)
    back = jnp.dot(member, fine_out, preferred_element_type=jnp.float32)
    diff = got_rows.astype(jnp.float32) - back
    row_error = jnp.sum(diff * diff, axis=1)
    spread = jnp.sum(member.astype(jnp.float32) * row_error[:, None], axis=0) / (
        width * (fine_counts + 1.0)
    )
    return (fine_out, middle_out.astype(jnp.bfloat16), third_out.astype(jnp.bfloat16), spread)


def solution(mesh):
    placed = (P(("dp", "clus"), None), P(("dp", "clus")), P(("dp", "clus")), P("dp"), P(), P())
    return jax.shard_map(
        local,
        mesh=mesh,
        in_specs=placed,
        out_specs=(
            P(("dp", "clus"), None),
            P(("dp", "clus"), None),
            P(("dp", "clus"), None),
            P(("dp", "clus")),
        ),
        check_vma=False,
    )
```

profile of v0, /device:TPU:0, one launch (start us, length us, event | category | flops | bytes accessed | tf_op | source)
XLA Modules:
  0.0 254.0 jit_solution(13841841108507027083)
XLA Ops:
  7.2 0.7 multiply_subtract_fusion
  7.9 0.2 fusion.5
  8.2 1.4 scatter_custom_fusion
  9.6 4.7 %gather_fusion = s32[512]{0:T(512)} fusion(s32[257]{0:T(512)S(1)} %pad_add_fusion, s32[1024]{0:T(1024)S(1)} %pad_clamp_fusion), kind=kCustom, calls=%fused_computation | custom fusion | bytes 6144 | tf_op jit(solution)/shard_map/gather | solution.py:46
  14.2 5.2 %all-to-all-start = ((s32[4,1,128]{2,1,0:T(1,128)}), s32[4,1,128]{2,1,0:T(1,128)S(1)}, u32[]{:S(2)}, u32[]{:S(2)}) async-start(s32[4,1,128]{2,1,0:T(1,128)} %bitcast), calls=%async_computation | async-start | bytes 4096 | tf_op jit(solution)/shard_map/all_to_all | solution.py:51
  19.5 2.8 %gather_fusion.1 = bf16[512,1024]{1,0:T(8,128)(2,1)} fusion(bf16[257,1024]{1,0:T(8,128)(2,1)S(1)} %concatenate.7, s32[1024]{0:T(1024)S(1)} %pad_clamp_fusion), kind=kCustom, calls=%fused_computation.1 | custom fusion | bytes 2099200 | tf_op jit(solution)/shard_map/gather | solution.py:45
  22.3 1.8 all-to-all-done
  24.0 3.5 %all-to-all-start.1 = ((bf16[4,128,1024]{2,1,0:T(8,128)(2,1)}), bf16[4,128,1024]{2,1,0:T(8,128)(2,1)S(1)}, u32[]{:S(2)}, u32[]{:S(2)}) async-start(bf16[4,128,1024]{2,1,0:T(8,128)(2,1)} %bitcast.2), calls=%async_computation.1 | async-start | bytes 2097152 | tf_op jit(solution)/shard_map/all_to_all | solution.py:50
  27.6 12.4 %all-to-all-done.1 = bf16[4,128,1024]{2,1,0:T(8,128)(2,1)S(1)} async-done(((bf16[4,128,1024]{2,1,0:T(8,128)(2,1)}), bf16[4,128,1024]{2,1,0:T(8,128)(2,1)S(1)}, u32[]{:S(2)}, u32[]{:S(2)}) %all-to-all-start.1) | async-done | bytes 1048608 | tf_op jit(solution)/shard_map/all_to_all | solution.py:50
  40.0 0.6 fusion.9
  40.7 1.7 fusion.15
  42.4 0.6 fusion.36
  45.0 0.6 dynamic-slice
  47.0 23.7 %reduce-scatter.2.cloned.1.call-done = f32[64,1024]{1,0:T(8,128)} async-done(((f32[256,1024]{1,0:T(8,128)}), f32[64,1024]{1,0:T(8,128)}) %reduce-scatter.2.cloned.1.call-update) | async-done | bytes 262160 | tf_op jit(solution)/shard_map/reduce_scatter | solution.py:66
  70.7 3.2 %fusion.13 = f32[512,1024]{1,0:T(8,128)} fusion(f32[64,1024]{1,0:T(8,128)} %reduce-scatter.2.cloned.1.call-done, s32[64]{0:T(128)S(1)} %dynamic_slice.6), kind=kOutput, calls=%fused_computation.26 | convolution fusion | flops 402685952 | bytes 2359552 | tf_op jit(solution)/shard_map/dot_general | solution.py:73
  74.0 0.1 convert_reduce_fusion
  74.2 0.2 fusion.14
  74.4 9.0 %all-reduce.1 = f32[256]{0:T(256)S(1)} all-reduce(f32[256]{0:T(256)S(1)} %bitcast.39), channel_id=3, replica_groups=mesh['dp'=8,'clus'=4] {'clus'}, use_global_device_ids=true, to_apply=%region_6.7.clone | all-reduce | flops 256 | bytes 2048
  83.4 0.2 fusion.12
  83.6 39.4 %psum.15 = f32[512]{0:T(512)S(1)} all-reduce(f32[512]{0:T(512)S(1)} %bitcast.38), channel_id=1, replica_groups=mesh['dp'=8,'clus'=4] {'dp','clus'}, use_global_device_ids=true, to_apply=%region_7.8 | all-reduce | flops 512 | bytes 4096 | tf_op jit(solution)/shard_map/psum | solution.py:75
  123.2 87.8 %all-reduce.4.cloned.1.call-done = f32[512,1024]{1,0:T(8,128)} async-done(((f32[512,1024]{1,0:T(8,128)}), f32[512,1024]{1,0:T(8,128)}) %all-reduce.4.cloned.1.call-update) | async-done | bytes 2097168 | tf_op jit(solution)/shard_map/psum | solution.py:75
  210.9 2.7 %fusion.37 = (f32[1024]{0:T(1024)S(1)}, f32[64,1024]{1,0:T(8,128)S(1)}) fusion(f32[512,1024]{1,0:T(8,128)} %all-reduce.4.cloned.1.call-done, s32[512]{0:T(512)S(1)} %copy-done.5), kind=kOutput, calls=%fused_computation.71 | convolution fusion | flops 402750464 | bytes 2365440 | tf_op jit(solution)/shard_map/dot_general | solution.py:77
  213.7 1.3 add_divide_fusion
  214.9 1.3 copy-done
  216.3 1.7 fusion.38
  218.0 0.7 broadcast_add_fusion.1
  218.7 1.5 dynamic-slice_convert_fusion
  220.1 23.3 %all-gather.2.cloned.1.call-done = f32[256,1024]{1,0:T(8,128)} async-done(((f32[64,1024]{1,0:T(8,128)}), f32[256,1024]{1,0:T(8,128)}) %all-gather.2.cloned.1.call-update) | async-done | bytes 1048592 | tf_op jit(solution)/shard_map/all_gather | solution.py:89
  243.4 2.6 %fusion.2 = bf16[256,1024]{1,0:T(8,128)(2,1)S(1)} fusion(f32[256,1024]{1,0:T(8,128)S(1)} %fusion.9, f32[256,1024]{1,0:T(8,128)} %all-gather.2.cloned.1.call-done, f32[256]{0:T(256)S(1)} %broadcast_add_fusion.1, f32[]{:T(128)} %bitcast.4, s32[256]{0:T(256)S(1)} %broadcast_subtract_fusion), kind=kOutput, calls=%fused_computation.8 | convolution fusion | flops 806420480 | bytes 2623492 | tf_op jit(solution)/shard_map/dot_general | solution.py:91
  246.1 0.6 multiply_reduce_fusion
  246.6 0.2 fusion.7
  246.9 0.6 multiply_divide_fusion
  (37 shorter events, 0.6 us)
Async XLA Ops:
  7.2 12.3 %copy-start.3 = (bf16[256,1024]{1,0:T(8,128)(2,1)S(1)}, bf16[256,1024]{1,0:T(8,128)(2,1)}, u32[]{:S(2)}) copy-start(bf16[256,1024]{1,0:T(8,128)(2,1)} %param.6) | copy-start | bytes 1572868
  14.2 9.8 %all-to-all-start = ((s32[4,1,128]{2,1,0:T(1,128)}), s32[4,1,128]{2,1,0:T(1,128)S(1)}, u32[]{:S(2)}, u32[]{:S(2)}) async-start(s32[4,1,128]{2,1,0:T(1,128)} %bitcast), calls=%async_computation | async-start | bytes 4096 | tf_op jit(solution)/shard_map/all_to_all | solution.py:51
  22.3 5.3 %copy-start.6 = (s32[256]{0:T(256)S(1)}, s32[256]{0:T(256)}, u32[]{:S(2)}) copy-start(s32[256]{0:T(256)} %param.8) | copy-start | bytes 3076
  24.0 16.0 %all-to-all-start.1 = ((bf16[4,128,1024]{2,1,0:T(8,128)(2,1)}), bf16[4,128,1024]{2,1,0:T(8,128)(2,1)S(1)}, u32[]{:S(2)}, u32[]{:S(2)}) async-start(bf16[4,128,1024]{2,1,0:T(8,128)(2,1)} %bitcast.2), calls=%async_computation.1 | async-start | bytes 2097152 | tf_op jit(solution)/shard_map/all_to_all | solution.py:50
  27.6 43.2 %reduce-scatter.2.cloned.1.call-start = ((), (), s32[]{:S(2)}) async-start(), calls=%async_computation.3 | async-start | bytes 1310720 | tf_op jit(solution)/shard_map/reduce_scatter | solution.py:66
  40.6 1.8 copy-start.4
  40.6 4.4 %copy-start.9 = (u32[32]{0:T(128)S(1)}, u32[32]{0:T(128)}, u32[]{:S(2)}) copy-start(u32[32]{0:T(128)} %constant.74) | copy-start | bytes 388
  40.6 5.6 %copy-start.7 = (s32[256]{0:T(256)S(1)}, s32[256]{0:T(256)}, u32[]{:S(2)}) copy-start(s32[256]{0:T(256)} %param.9) | copy-start | bytes 3076
  42.4 168.6 %all-reduce.4.cloned.1.call-start = ((), (), s32[]{:S(2)}) async-start(), calls=%async_computation.4 | async-start | bytes 4194304 | tf_op jit(solution)/shard_map/psum | solution.py:75
  47.0 76.1 %copy-start.5 = (s32[512]{0:T(512)S(1)}, s32[512]{0:T(512)}, u32[]{:S(2)}) copy-start(s32[512]{0:T(512)} %param.10) | copy-start | bytes 6148
  74.0 169.4 %all-gather.2.cloned.1.call-start = ((), (), s32[]{:S(2)}) async-start(), calls=%async_computation.5 | async-start | bytes 1310720 | tf_op jit(solution)/shard_map/all_gather | solution.py:89
  210.9 2.7 %copy-start.1 = (f32[512,1024]{1,0:T(8,128)S(1)}, f32[512,1024]{1,0:T(8,128)}, u32[]{:S(2)}) copy-start(f32[512,1024]{1,0:T(8,128)} %all-reduce.4.cloned.1.call-done) | copy-start | bytes 6291460
  213.7 2.6 %copy-start.2 = (f32[64,1024]{1,0:T(8,128)S(1)}, f32[64,1024]{1,0:T(8,128)}, u32[]{:S(2)}) copy-start(f32[64,1024]{1,0:T(8,128)} %reduce-scatter.2.cloned.1.call-done) | copy-start | bytes 786436
  214.9 1.4 copy-start
  246.1 1.4 copy-start.8
Sparse Core Ops, SparseCore 0:
  42.5 28.1 reduce-scatter.1
  76.1 134.8 all-reduce.3
  218.1 25.2 all-gather.1
where the time goes:
time: 254 us
  waiting for transfers between devices  149 us (59%)
  blocking collectives  48.4 us (19%)
  between operations  17.3 us (7%)
  matrix products  15.1 us (6%)
  local copies, waits for them, and re-layouts  13 us (5%)
  starting transfers between devices  8.83 us (3%)
    psum x1, waiting for transfers between devices, local(): lax.psum((third_part, third_tally), ('dp', 'clus'))  87.8 us
    psum x1, blocking collectives, local(): lax.psum((third_part, third_tally), ('dp', 'clus'))  39.4 us
    reduce_scatter x1, waiting for transfers between devices, local(): lax.psum_scatter(middle_part, 'clus', scatter_dimension=0, tiled=True)  23.7 us
    all_gather x1, waiting for transfers between devices, local(): middle_means = lax.all_gather(middle_out, 'clus', axis=0, tiled=True)  23.3 us
    all_to_all x1, waiting for transfers between devices, local(): lax.all_to_all(send_rows, 'clus', split_axis=0, concat_axis=0, tiled=True)  12.4 us
    unnamed x1, blocking collectives  8.99 us
    all_to_all x1, starting transfers between devices, local(): lax.all_to_all(send_ids, 'clus', split_axis=0, concat_axis=0, tiled=True)  5.19 us
  transfers between devices with their start and end apart: 5, of which 5 were waited for; matrix products, arithmetic and copies ran while one was open for 3% of the time, Pallas kernels for 0%

commit v1 on v0

--- a/solution.py
+++ b/solution.py
@@ -86,7 +86,12 @@
     middle_out = shrunk(
         middle_sums, middle_counts, jnp.dot(parent_hot, third_means, precision=HIGH), weight_middle
     )
-    middle_means = lax.all_gather(middle_out, "clus", axis=0, tiled=True)
+    ring = [middle_out]
+    for hop in range(3):
+        ring.append(lax.ppermute(ring[-1], "clus", [(dev, (dev + 1) % 4) for dev in range(4)]))
+    middle_means = jnp.roll(
+        jnp.concatenate(ring[::-1], axis=0), (lax.axis_index("clus") + 1) * ring[0].shape[0], axis=0
+    )
     fine_means = shrunk(
         fine_sums, fine_counts, jnp.dot(child_hot.T, middle_means, precision=HIGH), weight_fine
     )

time: 254 us -> 249 us (0.980)
  waiting for transfers between devices: 149 us -> 144 us
    all_gather x1 -> x0, waiting for transfers between devices: 23.3 us -> none  [local(): middle_means = lax.all_gather(middle_out, 'clus', axis=0, tiled=True)]
    ppermute x0 -> x3, waiting for transfers between devices: none -> 18.3 us  [local(): lax.ppermute(ring[-1], 'clus', [(dev, (dev + 1) % 4) for dev in range(4)])]
  transfers between devices with their start and end apart: 5 -> 7, of which waited for: 5 -> 7; matrix products, arithmetic and copies ran while one was open for 3% -> 3% of each run, Pallas kernels for 0% -> 0%
where the time goes in v1:
time: 249 us
  waiting for transfers between devices  144 us (58%)
  blocking collectives  48.4 us (19%)
  between operations  17.6 us (7%)
  matrix products  13 us (5%)
  local copies, waits for them, and re-layouts  11.8 us (5%)
  starting transfers between devices  10.7 us (4%)
  other arithmetic  3.15 us (1%)
    psum x1, waiting for transfers between devices, local(): lax.psum((third_part, third_tally), ('dp', 'clus'))  87.8 us
    psum x1, blocking collectives, local(): lax.psum((third_part, third_tally), ('dp', 'clus'))  39.4 us
    reduce_scatter x1, waiting for transfers between devices, local(): lax.psum_scatter(middle_part, 'clus', scatter_dimension=0, tiled=True)  23.7 us
    ppermute x3, waiting for transfers between devices, local(): lax.ppermute(ring[-1], 'clus', [(dev, (dev + 1) % 4) for dev in range(4)])  18.3 us
    all_to_all x1, waiting for transfers between devices, local(): lax.all_to_all(send_rows, 'clus', split_axis=0, concat_axis=0, tiled=True)  12.4 us
    unnamed x1, blocking collectives  8.99 us
    all_to_all x1, starting transfers between devices, local(): lax.all_to_all(send_ids, 'clus', split_axis=0, concat_axis=0, tiled=True)  5.19 us
  transfers between devices with their start and end apart: 7, of which 7 were waited for; matrix products, arithmetic and copies ran while one was open for 3% of the time, Pallas kernels for 0%

profile of v1, /device:TPU:0, one launch (start us, length us, event | category | flops | bytes accessed | tf_op | source)
XLA Modules:
  0.0 248.6 jit_solution(2208749577265552747)
XLA Ops:
  7.2 0.7 multiply_subtract_fusion
  8.2 1.4 scatter_custom_fusion
  9.6 4.7 %gather_fusion = s32[512]{0:T(512)} fusion(s32[257]{0:T(512)S(1)} %pad_add_fusion, s32[1024]{0:T(1024)S(1)} %pad_clamp_fusion), kind=kCustom, calls=%fused_computation | custom fusion | bytes 6144 | tf_op jit(solution)/shard_map/gather | solution.py:46
  14.2 5.2 %all-to-all-start = ((s32[4,1,128]{2,1,0:T(1,128)}), s32[4,1,128]{2,1,0:T(1,128)S(1)}, u32[]{:S(2)}, u32[]{:S(2)}) async-start(s32[4,1,128]{2,1,0:T(1,128)} %bitcast), calls=%async_computation | async-start | bytes 4096 | tf_op jit(solution)/shard_map/all_to_all | solution.py:51
  19.5 2.8 %gather_fusion.1 = bf16[512,1024]{1,0:T(8,128)(2,1)} fusion(bf16[257,1024]{1,0:T(8,128)(2,1)S(1)} %concatenate.13, s32[1024]{0:T(1024)S(1)} %pad_clamp_fusion), kind=kCustom, calls=%fused_computation.1 | custom fusion | bytes 2099200 | tf_op jit(solution)/shard_map/gather | solution.py:45
  22.3 1.8 all-to-all-done
  24.0 3.5 %all-to-all-start.1 = ((bf16[4,128,1024]{2,1,0:T(8,128)(2,1)}), bf16[4,128,1024]{2,1,0:T(8,128)(2,1)S(1)}, u32[]{:S(2)}, u32[]{:S(2)}) async-start(bf16[4,128,1024]{2,1,0:T(8,128)(2,1)} %bitcast.2), calls=%async_computation.1 | async-start | bytes 2097152 | tf_op jit(solution)/shard_map/all_to_all | solution.py:50
  27.6 12.4 %all-to-all-done.1 = bf16[4,128,1024]{2,1,0:T(8,128)(2,1)S(1)} async-done(((bf16[4,128,1024]{2,1,0:T(8,128)(2,1)}), bf16[4,128,1024]{2,1,0:T(8,128)(2,1)S(1)}, u32[]{:S(2)}, u32[]{:S(2)}) %all-to-all-start.1) | async-done | bytes 1048608 | tf_op jit(solution)/shard_map/all_to_all | solution.py:50
  40.0 0.6 fusion.10
  40.6 1.7 fusion.16
  42.4 0.6 fusion.39
  44.3 0.6 dynamic-slice
  47.0 23.7 %reduce-scatter.2.cloned.1.call-done = f32[64,1024]{1,0:T(8,128)} async-done(((f32[256,1024]{1,0:T(8,128)}), f32[64,1024]{1,0:T(8,128)}) %reduce-scatter.2.cloned.1.call-update) | async-done | bytes 262160 | tf_op jit(solution)/shard_map/reduce_scatter | solution.py:66
  70.7 3.2 %fusion.14 = f32[512,1024]{1,0:T(8,128)} fusion(f32[64,1024]{1,0:T(8,128)} %reduce-scatter.2.cloned.1.call-done, s32[64]{0:T(128)S(1)} %dynamic_slice.10), kind=kOutput, calls=%fused_computation.27 | convolution fusion | flops 402685952 | bytes 2359552 | tf_op jit(solution)/shard_map/dot_general | solution.py:73
  74.3 9.0 %all-reduce.1 = f32[256]{0:T(256)S(1)} all-reduce(f32[256]{0:T(256)S(1)} %bitcast.39), channel_id=3, replica_groups=mesh['dp'=8,'clus'=4] {'clus'}, use_global_device_ids=true, to_apply=%region_6.7.clone | all-reduce | flops 256 | bytes 2048
  83.3 0.2 fusion.13
  83.5 39.4 %psum.15 = f32[512]{0:T(512)S(1)} all-reduce(f32[512]{0:T(512)S(1)} %bitcast.38), channel_id=1, replica_groups=mesh['dp'=8,'clus'=4] {'dp','clus'}, use_global_device_ids=true, to_apply=%region_7.8 | all-reduce | flops 512 | bytes 4096 | tf_op jit(solution)/shard_map/psum | solution.py:75
  123.1 87.8 %all-reduce.4.cloned.1.call-done = f32[512,1024]{1,0:T(8,128)} async-done(((f32[512,1024]{1,0:T(8,128)}), f32[512,1024]{1,0:T(8,128)}) %all-reduce.4.cloned.1.call-update) | async-done | bytes 2097168 | tf_op jit(solution)/shard_map/psum | solution.py:75
  210.9 2.7 %fusion.40 = (f32[1024]{0:T(1024)S(1)}, f32[64,1024]{1,0:T(8,128)S(1)}) fusion(f32[512,1024]{1,0:T(8,128)} %all-reduce.4.cloned.1.call-done, s32[512]{0:T(512)S(1)} %copy-done.5), kind=kOutput, calls=%fused_computation.82 | convolution fusion | flops 402750464 | bytes 2365440 | tf_op jit(solution)/shard_map/dot_general | solution.py:77
  213.7 1.2 add_divide_fusion
  214.9 1.0 fusion.4
  215.8 1.3 collective-permute-start
  217.2 6.4 %collective-permute-done = f32[64,1024]{1,0:T(8,128)S(1)} collective-permute-done((f32[64,1024]{1,0:T(8,128)S(1)}, f32[64,1024]{1,0:T(8,128)S(1)}, u32[]{:S(2)}, u32[]{:S(2)}) %collective-permute-start) | collective-permute-done | bytes 262176 | tf_op jit(solution)/shard_map/ppermute | solution.py:91
  223.6 0.6 collective-permute-start.1
  224.2 6.7 %collective-permute-done.1 = f32[64,1024]{1,0:T(8,128)S(1)} collective-permute-done((f32[64,1024]{1,0:T(8,128)S(1)}, f32[64,1024]{1,0:T(8,128)S(1)}, u32[]{:S(2)}, u32[]{:S(2)}) %collective-permute-start.1) | collective-permute-done | bytes 262176 | tf_op jit(solution)/shard_map/ppermute | solution.py:91
  230.9 0.6 broadcast_add_fusion.1
  231.5 1.5 dynamic-slice_convert_fusion
  233.0 5.1 %collective-permute-done.2 = f32[64,1024]{1,0:T(8,128)S(1)} collective-permute-done((f32[64,1024]{1,0:T(8,128)S(1)}, f32[64,1024]{1,0:T(8,128)S(1)}, u32[]{:S(2)}, u32[]{:S(2)}) %collective-permute-start.2) | collective-permute-done | bytes 262176 | tf_op jit(solution)/shard_map/ppermute | solution.py:91
  238.2 0.7 fusion.38
  239.0 1.4 fusion.2
  240.4 0.6 multiply_reduce_fusion
  241.2 0.6 multiply_divide_fusion
  (48 shorter events, 1.4 us)
Async XLA Ops:
  7.2 12.3 %copy-start.3 = (bf16[256,1024]{1,0:T(8,128)(2,1)S(1)}, bf16[256,1024]{1,0:T(8,128)(2,1)}, u32[]{:S(2)}) copy-start(bf16[256,1024]{1,0:T(8,128)(2,1)} %param.6) | copy-start | bytes 1572868
  14.2 9.8 %all-to-all-start = ((s32[4,1,128]{2,1,0:T(1,128)}), s32[4,1,128]{2,1,0:T(1,128)S(1)}, u32[]{:S(2)}, u32[]{:S(2)}) async-start(s32[4,1,128]{2,1,0:T(1,128)} %bitcast), calls=%async_computation | async-start | bytes 4096 | tf_op jit(solution)/shard_map/all_to_all | solution.py:51
  22.3 5.3 %copy-start.6 = (s32[256]{0:T(256)S(1)}, s32[256]{0:T(256)}, u32[]{:S(2)}) copy-start(s32[256]{0:T(256)} %param.8) | copy-start | bytes 3076
  24.0 16.0 %all-to-all-start.1 = ((bf16[4,128,1024]{2,1,0:T(8,128)(2,1)}), bf16[4,128,1024]{2,1,0:T(8,128)(2,1)S(1)}, u32[]{:S(2)}, u32[]{:S(2)}) async-start(bf16[4,128,1024]{2,1,0:T(8,128)(2,1)} %bitcast.2), calls=%async_computation.1 | async-start | bytes 2097152 | tf_op jit(solution)/shard_map/all_to_all | solution.py:50
  27.6 43.2 %reduce-scatter.2.cloned.1.call-start = ((), (), s32[]{:S(2)}) async-start(), calls=%async_computation.3 | async-start | bytes 1310720 | tf_op jit(solution)/shard_map/reduce_scatter | solution.py:66
  40.6 1.8 copy-start.4
  40.6 3.7 %copy-start.9 = (u32[32]{0:T(128)S(1)}, u32[32]{0:T(128)}, u32[]{:S(2)}) copy-start(u32[32]{0:T(128)} %constant.94) | copy-start | bytes 388
  40.6 4.9 %copy-start.7 = (s32[256]{0:T(256)S(1)}, s32[256]{0:T(256)}, u32[]{:S(2)}) copy-start(s32[256]{0:T(256)} %param.9) | copy-start | bytes 3076
  42.4 168.6 %all-reduce.4.cloned.1.call-start = ((), (), s32[]{:S(2)}) async-start(), calls=%async_computation.4 | async-start | bytes 4194304 | tf_op jit(solution)/shard_map/psum | solution.py:75
  47.0 76.0 %copy-start.5 = (s32[512]{0:T(512)S(1)}, s32[512]{0:T(512)}, u32[]{:S(2)}) copy-start(s32[512]{0:T(512)} %param.10) | copy-start | bytes 6148
  210.9 2.7 %copy-start.1 = (f32[512,1024]{1,0:T(8,128)S(1)}, f32[512,1024]{1,0:T(8,128)}, u32[]{:S(2)}) copy-start(f32[512,1024]{1,0:T(8,128)} %all-reduce.4.cloned.1.call-done) | copy-start | bytes 6291460
  213.7 1.2 copy-start.2
  214.9 8.7 %copy-start = (f32[512,1024]{1,0:T(8,128)}, f32[512,1024]{1,0:T(8,128)S(1)}, u32[]{:S(2)}) copy-start(f32[512,1024]{1,0:T(8,128)S(1)} %add_divide_fusion) | copy-start | bytes 6291460
  215.8 7.8 %collective-permute-start = (f32[64,1024]{1,0:T(8,128)S(1)}, f32[64,1024]{1,0:T(8,128)S(1)}, u32[]{:S(2)}, u32[]{:S(2)}) collective-permute-start(f32[64,1024]{1,0:T(8,128)S(1)} %fusion.4), channel_id=1, source_target_pairs={{0,1},{1,2},{2,3},{3,0},{4,5},{5,6},{6,7},{7,4},{8,9},{9,10},{10,1... | collective-permute-start | bytes 786440 | tf_op jit(solution)/shard_map/ppermute | solution.py:91
  223.6 7.3 %collective-permute-start.1 = (f32[64,1024]{1,0:T(8,128)S(1)}, f32[64,1024]{1,0:T(8,128)S(1)}, u32[]{:S(2)}, u32[]{:S(2)}) collective-permute-start(f32[64,1024]{1,0:T(8,128)S(1)} %collective-permute-done), channel_id=1, source_target_pairs={{0,1},{1,2},{2,3},{3,0},{4,5},{5,6},{6,7},{7,4},{8,9},{9,10},{10,1... | collective-permute-start | bytes 786440 | tf_op jit(solution)/shard_map/ppermute | solution.py:91
  230.9 7.3 %collective-permute-start.2 = (f32[64,1024]{1,0:T(8,128)S(1)}, f32[64,1024]{1,0:T(8,128)S(1)}, u32[]{:S(2)}, u32[]{:S(2)}) collective-permute-start(f32[64,1024]{1,0:T(8,128)S(1)} %collective-permute-done.1), channel_id=1, source_target_pairs={{0,1},{1,2},{2,3},{3,0},{4,5},{5,6},{6,7},{7,4},{8,9},{9,10},{10,1... | collective-permute-start | bytes 786440 | tf_op jit(solution)/shard_map/ppermute | solution.py:91
  240.4 1.4 copy-start.8
Sparse Core Ops, SparseCore 0:
  42.5 28.1 reduce-scatter.1
  76.1 134.8 all-reduce.3
